TPU v7x, 256 devices: a whole 4x4x8 slice. The times are simulated.
256 devices in a mesh: section: 8 (over z_lo, core), dp: 32 (over y, x, z_hi).
Axes of the slice: x: 4, y: 4, z: 8 (z_hi: 2, z_lo: 4; z = z_hi * 4 + z_lo), core: 2. Of those that a mesh axis runs over, the one named last changes fastest.
Arguments:
- clips: bfloat16 [8, 32, 4, 8, 8, 128], P(None, 'dp'), may hold values from -6 to 6
- cotangent: bfloat16 [8, 32, 4, 8, 8, 128], P(None, 'dp'), may hold values from -6 to 6
- weights: bfloat16 [8, 3456, 128], P('section', 'dp'), may hold values from -0.078125 to 0.078125
Outputs:
- section_outs: bfloat16 [8, 8, 32, 4, 8, 8, 128], P('section', None, 'dp')
- weight_grads: float32 [8, 3456, 128], P('section', 'dp')
All inputs are finite; a program needn't handle non-finite values.
Results may differ from a plain program's by a relative error of at most 0.027.
Values may be sent and summed in bfloat16 or wider, within the bound.
A program may use at most 64 MiB of HBM per device.

v0:
```python
import jax
import jax.numpy as jnp
from jax import lax
from jax.sharding import PartitionSpec as P


def passed_along(block, axis, distance):
    devices = range(lax.axis_size(axis))
    route = [(i - distance, i) for i in devices if i - distance in devices]
    return lax.ppermute(block, axis, route)


def gather_patches(field):
    frames, height, width, channels = field.shape
    first_frame = field[:1]
    padded = jnp.concatenate([first_frame, first_frame, field], axis=0)
    padded = jnp.pad(padded, ((0, 0), (1, 1), (1, 1), (0, 0)))
    pieces = [
        padded[
            offset_time : offset_time + frames,
            offset_row : offset_row + height,
            offset_col : offset_col + width,
        ]
        for offset_time in range(3)
        for offset_row in range(3)
        for offset_col in range(3)
    ]
    return jnp.stack(pieces, axis=3).reshape(frames * height * width, 27 * channels)


def squash_field(activation):
    return jax.nn.silu(activation.astype(jnp.float32)).astype(jnp.bfloat16)


def squash_columns(activation):
    return gather_patches(squash_field(activation))


def layer_forward(activation, weight):
    branch = jnp.dot(squash_columns(activation), weight, preferred_element_type=jnp.float32)
    return (activation.astype(jnp.float32) + branch.reshape(activation.shape)).astype(jnp.bfloat16)


def input_gradient(activation, upstream, weight):
    flat_grad = upstream.reshape(-1, weight.shape[1])
    column_grad = lax.dot_general(
        flat_grad, weight, (((1,), (1,)), ((), ())), preferred_element_type=jnp.float32
    )
    base = activation.astype(jnp.float32)
    _, unfold = jax.vjp(gather_patches, base)
    field_grad = unfold(column_grad)[0]
    sigmoid_value = jax.nn.sigmoid(base)
    slope = sigmoid_value * (1.0 + base * (1.0 - sigmoid_value))
    return (upstream.astype(jnp.float32) + field_grad * slope).astype(jnp.bfloat16)


def weight_term(activation, upstream):
    flat_grad = upstream.reshape(-1, upstream.shape[-1])
    return lax.dot_general(
        squash_columns(activation),
        flat_grad,
        (((0,), (0,)), ((), ())),
        preferred_element_type=jnp.float32,
    )


def per_device(clips, cotangent, weights):
    section_total = lax.axis_size("section")
    section_index = lax.axis_index("section")
    weight = lax.all_gather(weights, "dp", axis=1, tiled=True)[0]
    local_clips = clips[:, 0]
    local_grads = cotangent[:, 0]
    micro_count = local_clips.shape[0]
    step_count = micro_count + section_total - 1
    empty_field = jnp.zeros(local_clips.shape[1:], jnp.bfloat16)

    def forward_step(step_index, carry):
        received, saved_inputs, produced = carry
        micro_index = step_index - section_index
        active = (micro_index >= 0) & (micro_index < micro_count)
        slot_index = jnp.clip(micro_index, 0, micro_count - 1)
        fresh = lax.dynamic_index_in_dim(local_clips, slot_index, 0, keepdims=False)
        layer_input = jnp.where(section_index == 0, fresh, received)
        layer_output = layer_forward(layer_input, weight)
        kept_input = jnp.where(
            active,
            layer_input,
            lax.dynamic_index_in_dim(saved_inputs, slot_index, 0, keepdims=False),
        )
        kept_output = jnp.where(
            active, layer_output, lax.dynamic_index_in_dim(produced, slot_index, 0, keepdims=False)
        )
        saved_inputs = lax.dynamic_update_index_in_dim(saved_inputs, kept_input, slot_index, 0)
        produced = lax.dynamic_update_index_in_dim(produced, kept_output, slot_index, 0)
        received = passed_along(layer_output, "section", 1)
        return (received, saved_inputs, produced)

    start_forward = (empty_field, jnp.zeros_like(local_clips), jnp.zeros_like(local_clips))
    _, saved_inputs, produced = lax.fori_loop(0, step_count, forward_step, start_forward)

    def backward_step(step_index, carry):
        received, grad_total, kept_grads = carry
        micro_index = step_index - (section_total - 1 - section_index)
        active = (micro_index >= 0) & (micro_index < micro_count)
        slot_index = jnp.clip(micro_index, 0, micro_count - 1)
        fresh = lax.dynamic_index_in_dim(local_grads, slot_index, 0, keepdims=False)
        upstream = jnp.where(section_index == section_total - 1, fresh, received)
        activation = lax.dynamic_index_in_dim(saved_inputs, slot_index, 0, keepdims=False)
        grad_total = grad_total + jnp.where(active, weight_term(activation, upstream), 0.0)
        layer_grad = input_gradient(activation, upstream, weight)
        received = passed_along(layer_grad, "section", -1)
        return (received, grad_total, kept_grads)

    start_backward = (
        empty_field,
        jnp.zeros(weight.shape, jnp.float32),
        jnp.zeros_like(local_grads),
    )
    _, grad_total, kept_grads = lax.fori_loop(0, step_count, backward_step, start_backward)
    grad_share = lax.psum_scatter(
        grad_total.astype(jnp.bfloat16), "dp", scatter_dimension=0, tiled=True
    ).astype(jnp.float32)
    return (produced[None, :, None], grad_share[None])


def solution(mesh):
    placed = (
        P(None, "dp", None, None, None, None),
        P(None, "dp", None, None, None, None),
        P("section", "dp", None),
    )
    return jax.shard_map(
        per_device,
        mesh=mesh,
        in_specs=placed,
        out_specs=(P("section", None, "dp", None, None, None, None), P("section", "dp", None)),
        check_vma=False,
    )
```

profile of v0, /device:TPU:98, one launch (start us, length us, event | category | flops | bytes accessed | tf_op | source)
XLA Modules:
  0.0 626.4 jit_solution(11397557660246506297)
XLA Ops:
  1.4 153.5 %all_gather.3 = bf16[1,3456,128]{2,0,1:T(2,128)(2,1)S(1)} all-gather(bf16[1,108,128]{2,0,1:T(2,128)(2,1)S(1)} %copy.118), channel_id=1, replica_groups=mesh['section'=8,'dp'=32] {'dp'}, dimensions={1}, use_global_device_ids=true | all-gather | bytes 912384 | tf_op jit(solution)/shard_map/all_gather | solution.py:70
  157.0 159.6 %while.37 = (s32[]{:T(128)}, bf16[4,8,8,128]{3,2,1,0:T(8,128)(2,1)S(1)}, bf16[8,4,8,8,128]{4,3,2,1,0:T(8,128)(2,1)}, bf16[8,4,8,8,128]{4,3,2,1,0:T(8,128)(2,1)S(...) while((s32[]{:T(128)}, ...), condition=%wide.region_1.2_spmd, body=%wide.region_0.1_spmd.sunk | while | flops 227311616 | bytes 8454884 | solution.py:99
  164.0 3.7 collective-permute-done
  174.7 3.7 collective-permute-done
  185.3 3.7 collective-permute-done
  196.0 3.7 collective-permute-done
  206.6 3.7 collective-permute-done
  217.3 3.7 collective-permute-done
  227.9 3.7 collective-permute-done
  238.5 3.7 collective-permute-done
  249.2 3.7 collective-permute-done
  259.8 3.7 collective-permute-done
  270.4 3.7 collective-permute-done
  281.1 3.7 collective-permute-done
  291.7 3.7 collective-permute-done
  302.3 3.7 collective-permute-done
  313.0 3.7 collective-permute-done
  317.4 174.1 %while.38 = (s32[]{:T(128)}, bf16[4,8,8,128]{3,2,1,0:T(8,128)(2,1)}, f32[3456,128]{1,0:T(8,128)S(1)}, pred[]{:T(512)}, s32[]{:T(128)}, /*index=5*/bf16[8,4,8,8,1...) while((s32[]{:T(128)}, ...), condition=%wide.region_3.4_spmd.clone, body=%wide.region_2.3_spmd.clone.sunk | while | flops 457267200 | bytes 30126344 | solution.py:119
  322.7 3.1 collective-permute-start.1
  327.8 2.0 fusion.264
  335.2 4.8 collective-permute-start.1
  342.0 2.0 fusion.264
  353.3 2.0 fusion.264
  360.7 2.6 collective-permute-start.1
  365.3 2.0 fusion.264
  387.9 2.0 fusion.264
  410.5 2.0 fusion.264
  444.4 2.0 fusion.264
  466.9 2.0 fusion.264
  489.5 2.0 fusion.264
  491.7 123.0 %fusion = bf16[112,128]{1,0:T(8,128)(2,1)S(1)} fusion(bf16[3456,128]{1,0:T(8,128)(2,1)S(1)} %convert_element_type.115), kind=kCustom, calls=%all-reduce-scatter | all-reduce-scatter fusion | flops 458753 | bytes 914432
  619.8 4.5 collective-permute-done.3
  (1148 shorter events, 255.8 us)
Async XLA Ops:
  162.1 5.6 collective-permute-start
  172.8 5.6 collective-permute-start
  183.4 5.6 collective-permute-start
  194.0 5.6 collective-permute-start
  204.7 5.6 collective-permute-start
  215.3 5.6 collective-permute-start
  226.0 5.6 collective-permute-start
  236.6 5.6 collective-permute-start
  247.2 5.6 collective-permute-start
  257.9 5.6 collective-permute-start
  268.5 5.6 collective-permute-start
  279.1 5.6 collective-permute-start
  289.8 5.6 collective-permute-start
  300.4 5.6 collective-permute-start
  311.0 5.6 collective-permute-start
  322.7 7.1 %collective-permute-start.1 = (bf16[4,8,8,128]{3,2,1,0:T(8,128)(2,1)}, bf16[4,8,8,128]{3,2,1,0:T(8,128)(2,1)}, u32[]{:S(2)}, u32[]{:S(2)}) collective-permute-start(bf16[4,8,8,128]{3,2,1,0:T(8,128)(2,1)} %get-tuple-element.632), channel_id=1, source_target_pairs={{32,0},{64,32},{96,64},{128,96},{160,128},{192,160},{224,192},{33,... | collective-permute-start | bytes 196616 | tf_op jit(solution)/shard_map/while/body/eval_jaxpr/ppermute | solution.py:10
  335.2 8.9 %collective-permute-start.1 = (bf16[4,8,8,128]{3,2,1,0:T(8,128)(2,1)}, bf16[4,8,8,128]{3,2,1,0:T(8,128)(2,1)}, u32[]{:S(2)}, u32[]{:S(2)}) collective-permute-start(bf16[4,8,8,128]{3,2,1,0:T(8,128)(2,1)} %get-tuple-element.632), channel_id=1, source_target_pairs={{32,0},{64,32},{96,64},{128,96},{160,128},{192,160},{224,192},{33,... | collective-permute-start | bytes 196616 | tf_op jit(solution)/shard_map/while/body/eval_jaxpr/ppermute | solution.py:10
  349.4 6.0 collective-permute-start.1
  360.7 6.7 %collective-permute-start.1 = (bf16[4,8,8,128]{3,2,1,0:T(8,128)(2,1)}, bf16[4,8,8,128]{3,2,1,0:T(8,128)(2,1)}, u32[]{:S(2)}, u32[]{:S(2)}) collective-permute-start(bf16[4,8,8,128]{3,2,1,0:T(8,128)(2,1)} %get-tuple-element.632), channel_id=1, source_target_pairs={{32,0},{64,32},{96,64},{128,96},{160,128},{192,160},{224,192},{33,... | collective-permute-start | bytes 196616 | tf_op jit(solution)/shard_map/while/body/eval_jaxpr/ppermute | solution.py:10
  372.7 6.0 collective-permute-start.1
  384.0 6.0 collective-permute-start.1
  395.3 6.0 collective-permute-start.1
  406.6 6.0 collective-permute-start.1
  417.8 6.0 collective-permute-start.1
  429.1 6.0 collective-permute-start.1
  440.4 6.0 collective-permute-start.1
  451.7 6.0 collective-permute-start.1
  463.0 6.0 collective-permute-start.1
  474.3 6.0 collective-permute-start.1
  485.6 6.0 collective-permute-start.1
  614.7 10.6 %collective-permute-start.2 = (bf16[112,128]{1,0:T(8,128)(2,1)S(1)}, bf16[112,128]{1,0:T(8,128)(2,1)S(1)}, u32[]{:S(2)}, u32[]{:S(2)}) collective-permute-start(bf16[112,128]{1,0:T(8,128)(2,1)S(1)} %fusion), channel_id=1, source_target_pairs={{0,1},{1,2},{2,3},{3,4},{4,5},{5,6},{6,7},{7,8},{8,9},{9,10},{10,1... | collective-permute-start | bytes 86024
  616.6 7.7 %collective-permute-start.3 = (bf16[12,128]{1,0:T(8,128)(2,1)S(1)}, bf16[12,128]{1,0:T(8,128)(2,1)S(1)}, u32[]{:S(2)}, u32[]{:S(2)}) collective-permute-start(bf16[12,128]{1,0:T(8,128)(2,1)S(1)} %slice.589), channel_id=1, source_target_pairs={{0,2},{1,3},{2,4},{3,5},{4,6},{5,7},{6,8},{7,9},{8,10},{9,11},{10,... | collective-permute-start | bytes 9224
  (17 other events, 170.4 us)
where the time goes:
time: 633 us; the launch traced here: 626 us
  blocking collectives  276 us (44%)
  matrix products  85.5 us (14%)
  other arithmetic  82.8 us (13%)
  starting transfers between devices  66.2 us (10%)
  waiting for transfers between devices  60.3 us (10%)
  local copies, waits for them, and re-layouts  49.3 us (8%)
    all_gather x1, blocking collectives, per_device(): weight = lax.all_gather(weights, 'dp', axis=1, tiled=True)[0]  153 us
    unnamed x1, blocking collectives  123 us
    ppermute x30, starting transfers between devices, passed_along(): return lax.ppermute(block, axis, route)  62.3 us
    ppermute x30, waiting for transfers between devices, passed_along(): return lax.ppermute(block, axis, route)  54.8 us
    dot_general x15, matrix products, weight_term(): lax.dot_general(squash_columns(activation), flat_grad, (((0,), (0,)), (()...  30.6 us
    dot_general x15, matrix products, layer_forward(): jnp.dot(squash_columns(activation), weight, preferred_element_type=jnp.fl...  27.5 us
    dot_general x15, matrix products, input_gradient(): lax.dot_general(flat_grad, weight, (((1,), (1,)), ((), ())), preferred_el...  27.4 us
    convert_element_type x30, other arithmetic, squash_field(): return jax.nn.silu(activation.astype(jnp.float32)).astype(jnp.bfloat16)  23.9 us
  transfers between devices with their start and end apart: 32, of which 17 were waited for; matrix products, arithmetic and copies ran while one was open for 10% of the time, Pallas kernels for 0%

commit v1 on v0

--- a/solution.py
+++ b/solution.py
@@ -67,7 +67,9 @@
 def per_device(clips, cotangent, weights):
     section_total = lax.axis_size("section")
     section_index = lax.axis_index("section")
-    weight = lax.all_gather(weights, "dp", axis=1, tiled=True)[0]
+    weight = jnp.concatenate(
+        lax.all_to_all(jnp.stack([weights] * lax.axis_size("dp")), "dp", 0, 0), axis=1
+    )[0]
     local_clips = clips[:, 0]
     local_grads = cotangent[:, 0]
     micro_count = local_clips.shape[0]

time: 633 us -> 517 us (0.82)
  blocking collectives: 276 us -> 121 us
  waiting for transfers between devices: 60.3 us -> 87.3 us
  starting transfers between devices: 66.2 us -> 77.1 us
    all_gather x1 -> x0, blocking collectives: 153 us -> none  [per_device(): weight = lax.all_gather(weights, 'dp', axis=1, tiled=True)[0]]
    all_to_all x0 -> x1, waiting for transfers between devices: none -> 21.6 us  [per_device(): lax.all_to_all(jnp.stack([weights] * lax.axis_size('dp')), 'dp', 0, 0)]
    all_to_all x0 -> x1, starting transfers between devices: none -> 11.5 us  [per_device(): lax.all_to_all(jnp.stack([weights] * lax.axis_size('dp')), 'dp', 0, 0)]
  transfers between devices with their start and end apart: 32 -> 33, of which waited for: 17 -> 18; matrix products, arithmetic and copies ran while one was open for 10% -> 12% of each run, Pallas kernels for 0% -> 0%
where the time goes in v1:
time: 517 us; the launch traced here: 510 us
  blocking collectives  121 us (23%)
  waiting for transfers between devices  87.3 us (17%)
  matrix products  85.5 us (17%)
  other arithmetic  82.7 us (16%)
  starting transfers between devices  77.1 us (15%)
  local copies, waits for them, and re-layouts  50.3 us (10%)
    unnamed x1, blocking collectives  121 us
    ppermute x30, starting transfers between devices, passed_along(): return lax.ppermute(block, axis, route)  61.7 us
    ppermute x30, waiting for transfers between devices, passed_along(): return lax.ppermute(block, axis, route)  60.1 us
    dot_general x15, matrix products, weight_term(): lax.dot_general(squash_columns(activation), flat_grad, (((0,), (0,)), (()...  30.6 us
    dot_general x15, matrix products, layer_forward(): jnp.dot(squash_columns(activation), weight, preferred_element_type=jnp.fl...  27.5 us
    dot_general x15, matrix products, input_gradient(): lax.dot_general(flat_grad, weight, (((1,), (1,)), ((), ())), preferred_el...  27.4 us
    convert_element_type x30, other arithmetic, squash_field(): return jax.nn.silu(activation.astype(jnp.float32)).astype(jnp.bfloat16)  24 us
    dynamic_update_slice x15, other arithmetic, forward_step(): lax.dynamic_update_index_in_dim(saved_inputs, kept_input, slot_index, 0)  22.4 us
  transfers between devices with their start and end apart: 33, of which 18 were waited for; matrix products, arithmetic and copies ran while one was open for 12% of the time, Pallas kernels for 0%

profile of v1, /device:TPU:98, one launch (start us, length us, event | category | flops | bytes accessed | tf_op | source)
XLA Modules:
  0.0 510.2 jit_solution(8583848477120478737)
XLA Ops:
  2.4 11.5 %all-to-all-start = ((bf16[32,1,108,128]{3,2,1,0:T(8,128)(2,1)}), bf16[32,1,108,128]{3,2,1,0:T(8,128)(2,1)S(1)}, u32[]{:S(2)}, u32[]{:S(2)}) async-start(bf16[32,1,108,128]{3,2,1,0:T(8,128)(2,1)} %stack.591), calls=%async_computation | async-start | bytes 1835008 | tf_op jit(solution)/shard_map/all_to_all | solution.py:71
  14.0 21.6 %all-to-all-done = bf16[32,1,108,128]{3,2,1,0:T(8,128)(2,1)S(1)} async-done(((bf16[32,1,108,128]{3,2,1,0:T(8,128)(2,1)}), bf16[32,1,108,128]{3,2,1,0:T(8,128)(2,1)S(1)}, u32[]{:S(2)}, u32[]{:S(2)}) %all-to-all-start) | async-done | bytes 884768 | tf_op jit(solution)/shard_map/all_to_all | solution.py:71
  37.7 164.7 %while.37 = (s32[]{:T(128)}, bf16[4,8,8,128]{3,2,1,0:T(8,128)(2,1)S(1)}, bf16[8,4,8,8,128]{4,3,2,1,0:T(8,128)(2,1)}, bf16[8,4,8,8,128]{4,3,2,1,0:T(8,128)(2,1)S(...) while((s32[]{:T(128)}, ...), condition=%wide.region_1.2_spmd, body=%wide.region_0.1_spmd.sunk | while | flops 227311616 | bytes 8454884 | solution.py:101
  44.7 8.9 %collective-permute-done = bf16[4,8,8,128]{3,2,1,0:T(8,128)(2,1)S(1)} collective-permute-done((bf16[4,8,8,128]{3,2,1,0:T(8,128)(2,1)S(1)}, bf16[4,8,8,128]{3,2,1,0:T(8,128)(2,1)S(1)}, u32[]{:S(2)}, u32[]{:S(2)}) %collective-permute-start) | collective-permute-done | bytes 65568 | tf_op jit(solution)/shard_map/while/body/eval_jaxpr/ppermute | solution.py:10
  60.6 3.7 collective-permute-done
  71.3 3.7 collective-permute-done
  81.9 3.7 collective-permute-done
  92.5 3.7 collective-permute-done
  103.1 3.7 collective-permute-done
  113.8 3.7 collective-permute-done
  124.4 3.7 collective-permute-done
  135.0 3.7 collective-permute-done
  145.7 3.7 collective-permute-done
  156.3 3.7 collective-permute-done
  166.9 3.7 collective-permute-done
  177.6 3.7 collective-permute-done
  188.2 3.7 collective-permute-done
  198.8 3.7 collective-permute-done
  203.3 173.7 %while.38 = (s32[]{:T(128)}, bf16[4,8,8,128]{3,2,1,0:T(8,128)(2,1)}, f32[3456,128]{1,0:T(8,128)S(1)}, pred[]{:T(512)}, s32[]{:T(128)}, /*index=5*/bf16[8,4,8,8,1...) while((s32[]{:T(128)}, ...), condition=%wide.region_3.4_spmd.clone, body=%wide.region_2.3_spmd.clone.sunk | while | flops 457267200 | bytes 30126344 | solution.py:121
  208.6 2.1 collective-permute-start.1
  212.7 2.0 fusion.264
  220.1 4.8 collective-permute-start.1
  226.9 2.0 fusion.264
  238.2 2.0 fusion.264
  245.6 3.0 collective-permute-start.1
  250.6 2.0 fusion.264
  261.9 2.0 fusion.264
  284.5 2.0 fusion.264
  352.3 2.0 fusion.264
  363.6 2.0 fusion.264
  377.1 121.3 %fusion = bf16[112,128]{1,0:T(8,128)(2,1)S(1)} fusion(bf16[3456,128]{1,0:T(8,128)(2,1)S(1)} %convert_element_type.115), kind=kCustom, calls=%all-reduce-scatter | all-reduce-scatter fusion | flops 458753 | bytes 914432
  503.5 4.4 collective-permute-done.3
  (1149 shorter events, 259.0 us)
Async XLA Ops:
  2.4 33.2 %all-to-all-start = ((bf16[32,1,108,128]{3,2,1,0:T(8,128)(2,1)}), bf16[32,1,108,128]{3,2,1,0:T(8,128)(2,1)S(1)}, u32[]{:S(2)}, u32[]{:S(2)}) async-start(bf16[32,1,108,128]{3,2,1,0:T(8,128)(2,1)} %stack.591), calls=%async_computation | async-start | bytes 1835008 | tf_op jit(solution)/shard_map/all_to_all | solution.py:71
  42.8 10.9 %collective-permute-start = (bf16[4,8,8,128]{3,2,1,0:T(8,128)(2,1)S(1)}, bf16[4,8,8,128]{3,2,1,0:T(8,128)(2,1)S(1)}, u32[]{:S(2)}, u32[]{:S(2)}) collective-permute-start(bf16[4,8,8,128]{3,2,1,0:T(8,128)(2,1)S(1)} %get-tuple-element.592), channel_id=1, source_target_pairs={{0,32},{32,64},{64,96},{96,128},{128,160},{160,192},{192,224},{1,3... | collective-permute-start | bytes 196616 | tf_op jit(solution)/shard_map/while/body/eval_jaxpr/ppermute | solution.py:10
  58.7 5.6 %collective-permute-start = (bf16[4,8,8,128]{3,2,1,0:T(8,128)(2,1)S(1)}, bf16[4,8,8,128]{3,2,1,0:T(8,128)(2,1)S(1)}, u32[]{:S(2)}, u32[]{:S(2)}) collective-permute-start(bf16[4,8,8,128]{3,2,1,0:T(8,128)(2,1)S(1)} %get-tuple-element.592), channel_id=1, source_target_pairs={{0,32},{32,64},{64,96},{96,128},{128,160},{160,192},{192,224},{1,3... | collective-permute-start | bytes 196616 | tf_op jit(solution)/shard_map/while/body/eval_jaxpr/ppermute | solution.py:10
  69.3 5.6 %collective-permute-start = (bf16[4,8,8,128]{3,2,1,0:T(8,128)(2,1)S(1)}, bf16[4,8,8,128]{3,2,1,0:T(8,128)(2,1)S(1)}, u32[]{:S(2)}, u32[]{:S(2)}) collective-permute-start(bf16[4,8,8,128]{3,2,1,0:T(8,128)(2,1)S(1)} %get-tuple-element.592), channel_id=1, source_target_pairs={{0,32},{32,64},{64,96},{96,128},{128,160},{160,192},{192,224},{1,3... | collective-permute-start | bytes 196616 | tf_op jit(solution)/shard_map/while/body/eval_jaxpr/ppermute | solution.py:10
  80.0 5.6 %collective-permute-start = (bf16[4,8,8,128]{3,2,1,0:T(8,128)(2,1)S(1)}, bf16[4,8,8,128]{3,2,1,0:T(8,128)(2,1)S(1)}, u32[]{:S(2)}, u32[]{:S(2)}) collective-permute-start(bf16[4,8,8,128]{3,2,1,0:T(8,128)(2,1)S(1)} %get-tuple-element.592), channel_id=1, source_target_pairs={{0,32},{32,64},{64,96},{96,128},{128,160},{160,192},{192,224},{1,3... | collective-permute-start | bytes 196616 | tf_op jit(solution)/shard_map/while/body/eval_jaxpr/ppermute | solution.py:10
  90.6 5.6 %collective-permute-start = (bf16[4,8,8,128]{3,2,1,0:T(8,128)(2,1)S(1)}, bf16[4,8,8,128]{3,2,1,0:T(8,128)(2,1)S(1)}, u32[]{:S(2)}, u32[]{:S(2)}) collective-permute-start(bf16[4,8,8,128]{3,2,1,0:T(8,128)(2,1)S(1)} %get-tuple-element.592), channel_id=1, source_target_pairs={{0,32},{32,64},{64,96},{96,128},{128,160},{160,192},{192,224},{1,3... | collective-permute-start | bytes 196616 | tf_op jit(solution)/shard_map/while/body/eval_jaxpr/ppermute | solution.py:10
  101.2 5.6 %collective-permute-start = (bf16[4,8,8,128]{3,2,1,0:T(8,128)(2,1)S(1)}, bf16[4,8,8,128]{3,2,1,0:T(8,128)(2,1)S(1)}, u32[]{:S(2)}, u32[]{:S(2)}) collective-permute-start(bf16[4,8,8,128]{3,2,1,0:T(8,128)(2,1)S(1)} %get-tuple-element.592), channel_id=1, source_target_pairs={{0,32},{32,64},{64,96},{96,128},{128,160},{160,192},{192,224},{1,3... | collective-permute-start | bytes 196616 | tf_op jit(solution)/shard_map/while/body/eval_jaxpr/ppermute | solution.py:10
  111.8 5.6 %collective-permute-start = (bf16[4,8,8,128]{3,2,1,0:T(8,128)(2,1)S(1)}, bf16[4,8,8,128]{3,2,1,0:T(8,128)(2,1)S(1)}, u32[]{:S(2)}, u32[]{:S(2)}) collective-permute-start(bf16[4,8,8,128]{3,2,1,0:T(8,128)(2,1)S(1)} %get-tuple-element.592), channel_id=1, source_target_pairs={{0,32},{32,64},{64,96},{96,128},{128,160},{160,192},{192,224},{1,3... | collective-permute-start | bytes 196616 | tf_op jit(solution)/shard_map/while/body/eval_jaxpr/ppermute | solution.py:10
  122.5 5.6 %collective-permute-start = (bf16[4,8,8,128]{3,2,1,0:T(8,128)(2,1)S(1)}, bf16[4,8,8,128]{3,2,1,0:T(8,128)(2,1)S(1)}, u32[]{:S(2)}, u32[]{:S(2)}) collective-permute-start(bf16[4,8,8,128]{3,2,1,0:T(8,128)(2,1)S(1)} %get-tuple-element.592), channel_id=1, source_target_pairs={{0,32},{32,64},{64,96},{96,128},{128,160},{160,192},{192,224},{1,3... | collective-permute-start | bytes 196616 | tf_op jit(solution)/shard_map/while/body/eval_jaxpr/ppermute | solution.py:10
  133.1 5.6 %collective-permute-start = (bf16[4,8,8,128]{3,2,1,0:T(8,128)(2,1)S(1)}, bf16[4,8,8,128]{3,2,1,0:T(8,128)(2,1)S(1)}, u32[]{:S(2)}, u32[]{:S(2)}) collective-permute-start(bf16[4,8,8,128]{3,2,1,0:T(8,128)(2,1)S(1)} %get-tuple-element.592), channel_id=1, source_target_pairs={{0,32},{32,64},{64,96},{96,128},{128,160},{160,192},{192,224},{1,3... | collective-permute-start | bytes 196616 | tf_op jit(solution)/shard_map/while/body/eval_jaxpr/ppermute | solution.py:10
  143.7 5.6 %collective-permute-start = (bf16[4,8,8,128]{3,2,1,0:T(8,128)(2,1)S(1)}, bf16[4,8,8,128]{3,2,1,0:T(8,128)(2,1)S(1)}, u32[]{:S(2)}, u32[]{:S(2)}) collective-permute-start(bf16[4,8,8,128]{3,2,1,0:T(8,128)(2,1)S(1)} %get-tuple-element.592), channel_id=1, source_target_pairs={{0,32},{32,64},{64,96},{96,128},{128,160},{160,192},{192,224},{1,3... | collective-permute-start | bytes 196616 | tf_op jit(solution)/shard_map/while/body/eval_jaxpr/ppermute | solution.py:10
  154.4 5.6 %collective-permute-start = (bf16[4,8,8,128]{3,2,1,0:T(8,128)(2,1)S(1)}, bf16[4,8,8,128]{3,2,1,0:T(8,128)(2,1)S(1)}, u32[]{:S(2)}, u32[]{:S(2)}) collective-permute-start(bf16[4,8,8,128]{3,2,1,0:T(8,128)(2,1)S(1)} %get-tuple-element.592), channel_id=1, source_target_pairs={{0,32},{32,64},{64,96},{96,128},{128,160},{160,192},{192,224},{1,3... | collective-permute-start | bytes 196616 | tf_op jit(solution)/shard_map/while/body/eval_jaxpr/ppermute | solution.py:10
  165.0 5.6 %collective-permute-start = (bf16[4,8,8,128]{3,2,1,0:T(8,128)(2,1)S(1)}, bf16[4,8,8,128]{3,2,1,0:T(8,128)(2,1)S(1)}, u32[]{:S(2)}, u32[]{:S(2)}) collective-permute-start(bf16[4,8,8,128]{3,2,1,0:T(8,128)(2,1)S(1)} %get-tuple-element.592), channel_id=1, source_target_pairs={{0,32},{32,64},{64,96},{96,128},{128,160},{160,192},{192,224},{1,3... | collective-permute-start | bytes 196616 | tf_op jit(solution)/shard_map/while/body/eval_jaxpr/ppermute | solution.py:10
  175.6 5.6 %collective-permute-start = (bf16[4,8,8,128]{3,2,1,0:T(8,128)(2,1)S(1)}, bf16[4,8,8,128]{3,2,1,0:T(8,128)(2,1)S(1)}, u32[]{:S(2)}, u32[]{:S(2)}) collective-permute-start(bf16[4,8,8,128]{3,2,1,0:T(8,128)(2,1)S(1)} %get-tuple-element.592), channel_id=1, source_target_pairs={{0,32},{32,64},{64,96},{96,128},{128,160},{160,192},{192,224},{1,3... | collective-permute-start | bytes 196616 | tf_op jit(solution)/shard_map/while/body/eval_jaxpr/ppermute | solution.py:10
  186.3 5.6 %collective-permute-start = (bf16[4,8,8,128]{3,2,1,0:T(8,128)(2,1)S(1)}, bf16[4,8,8,128]{3,2,1,0:T(8,128)(2,1)S(1)}, u32[]{:S(2)}, u32[]{:S(2)}) collective-permute-start(bf16[4,8,8,128]{3,2,1,0:T(8,128)(2,1)S(1)} %get-tuple-element.592), channel_id=1, source_target_pairs={{0,32},{32,64},{64,96},{96,128},{128,160},{160,192},{192,224},{1,3... | collective-permute-start | bytes 196616 | tf_op jit(solution)/shard_map/while/body/eval_jaxpr/ppermute | solution.py:10
  208.6 6.2 %collective-permute-start.1 = (bf16[4,8,8,128]{3,2,1,0:T(8,128)(2,1)}, bf16[4,8,8,128]{3,2,1,0:T(8,128)(2,1)}, u32[]{:S(2)}, u32[]{:S(2)}) collective-permute-start(bf16[4,8,8,128]{3,2,1,0:T(8,128)(2,1)} %get-tuple-element.630), channel_id=1, source_target_pairs={{32,0},{64,32},{96,64},{128,96},{160,128},{192,160},{224,192},{33,... | collective-permute-start | bytes 196616 | tf_op jit(solution)/shard_map/while/body/eval_jaxpr/ppermute | solution.py:10
  220.1 8.9 %collective-permute-start.1 = (bf16[4,8,8,128]{3,2,1,0:T(8,128)(2,1)}, bf16[4,8,8,128]{3,2,1,0:T(8,128)(2,1)}, u32[]{:S(2)}, u32[]{:S(2)}) collective-permute-start(bf16[4,8,8,128]{3,2,1,0:T(8,128)(2,1)} %get-tuple-element.630), channel_id=1, source_target_pairs={{32,0},{64,32},{96,64},{128,96},{160,128},{192,160},{224,192},{33,... | collective-permute-start | bytes 196616 | tf_op jit(solution)/shard_map/while/body/eval_jaxpr/ppermute | solution.py:10
  234.3 6.0 %collective-permute-start.1 = (bf16[4,8,8,128]{3,2,1,0:T(8,128)(2,1)}, bf16[4,8,8,128]{3,2,1,0:T(8,128)(2,1)}, u32[]{:S(2)}, u32[]{:S(2)}) collective-permute-start(bf16[4,8,8,128]{3,2,1,0:T(8,128)(2,1)} %get-tuple-element.630), channel_id=1, source_target_pairs={{32,0},{64,32},{96,64},{128,96},{160,128},{192,160},{224,192},{33,... | collective-permute-start | bytes 196616 | tf_op jit(solution)/shard_map/while/body/eval_jaxpr/ppermute | solution.py:10
  245.6 7.1 %collective-permute-start.1 = (bf16[4,8,8,128]{3,2,1,0:T(8,128)(2,1)}, bf16[4,8,8,128]{3,2,1,0:T(8,128)(2,1)}, u32[]{:S(2)}, u32[]{:S(2)}) collective-permute-start(bf16[4,8,8,128]{3,2,1,0:T(8,128)(2,1)} %get-tuple-element.630), channel_id=1, source_target_pairs={{32,0},{64,32},{96,64},{128,96},{160,128},{192,160},{224,192},{33,... | collective-permute-start | bytes 196616 | tf_op jit(solution)/shard_map/while/body/eval_jaxpr/ppermute | solution.py:10
  258.0 6.0 %collective-permute-start.1 = (bf16[4,8,8,128]{3,2,1,0:T(8,128)(2,1)}, bf16[4,8,8,128]{3,2,1,0:T(8,128)(2,1)}, u32[]{:S(2)}, u32[]{:S(2)}) collective-permute-start(bf16[4,8,8,128]{3,2,1,0:T(8,128)(2,1)} %get-tuple-element.630), channel_id=1, source_target_pairs={{32,0},{64,32},{96,64},{128,96},{160,128},{192,160},{224,192},{33,... | collective-permute-start | bytes 196616 | tf_op jit(solution)/shard_map/while/body/eval_jaxpr/ppermute | solution.py:10
  269.3 6.0 %collective-permute-start.1 = (bf16[4,8,8,128]{3,2,1,0:T(8,128)(2,1)}, bf16[4,8,8,128]{3,2,1,0:T(8,128)(2,1)}, u32[]{:S(2)}, u32[]{:S(2)}) collective-permute-start(bf16[4,8,8,128]{3,2,1,0:T(8,128)(2,1)} %get-tuple-element.630), channel_id=1, source_target_pairs={{32,0},{64,32},{96,64},{128,96},{160,128},{192,160},{224,192},{33,... | collective-permute-start | bytes 196616 | tf_op jit(solution)/shard_map/while/body/eval_jaxpr/ppermute | solution.py:10
  280.6 6.0 %collective-permute-start.1 = (bf16[4,8,8,128]{3,2,1,0:T(8,128)(2,1)}, bf16[4,8,8,128]{3,2,1,0:T(8,128)(2,1)}, u32[]{:S(2)}, u32[]{:S(2)}) collective-permute-start(bf16[4,8,8,128]{3,2,1,0:T(8,128)(2,1)} %get-tuple-element.630), channel_id=1, source_target_pairs={{32,0},{64,32},{96,64},{128,96},{160,128},{192,160},{224,192},{33,... | collective-permute-start | bytes 196616 | tf_op jit(solution)/shard_map/while/body/eval_jaxpr/ppermute | solution.py:10
  291.9 6.0 %collective-permute-start.1 = (bf16[4,8,8,128]{3,2,1,0:T(8,128)(2,1)}, bf16[4,8,8,128]{3,2,1,0:T(8,128)(2,1)}, u32[]{:S(2)}, u32[]{:S(2)}) collective-permute-start(bf16[4,8,8,128]{3,2,1,0:T(8,128)(2,1)} %get-tuple-element.630), channel_id=1, source_target_pairs={{32,0},{64,32},{96,64},{128,96},{160,128},{192,160},{224,192},{33,... | collective-permute-start | bytes 196616 | tf_op jit(solution)/shard_map/while/body/eval_jaxpr/ppermute | solution.py:10
  303.2 6.0 %collective-permute-start.1 = (bf16[4,8,8,128]{3,2,1,0:T(8,128)(2,1)}, bf16[4,8,8,128]{3,2,1,0:T(8,128)(2,1)}, u32[]{:S(2)}, u32[]{:S(2)}) collective-permute-start(bf16[4,8,8,128]{3,2,1,0:T(8,128)(2,1)} %get-tuple-element.630), channel_id=1, source_target_pairs={{32,0},{64,32},{96,64},{128,96},{160,128},{192,160},{224,192},{33,... | collective-permute-start | bytes 196616 | tf_op jit(solution)/shard_map/while/body/eval_jaxpr/ppermute | solution.py:10
  314.5 6.0 %collective-permute-start.1 = (bf16[4,8,8,128]{3,2,1,0:T(8,128)(2,1)}, bf16[4,8,8,128]{3,2,1,0:T(8,128)(2,1)}, u32[]{:S(2)}, u32[]{:S(2)}) collective-permute-start(bf16[4,8,8,128]{3,2,1,0:T(8,128)(2,1)} %get-tuple-element.630), channel_id=1, source_target_pairs={{32,0},{64,32},{96,64},{128,96},{160,128},{192,160},{224,192},{33,... | collective-permute-start | bytes 196616 | tf_op jit(solution)/shard_map/while/body/eval_jaxpr/ppermute | solution.py:10
  325.8 6.0 %collective-permute-start.1 = (bf16[4,8,8,128]{3,2,1,0:T(8,128)(2,1)}, bf16[4,8,8,128]{3,2,1,0:T(8,128)(2,1)}, u32[]{:S(2)}, u32[]{:S(2)}) collective-permute-start(bf16[4,8,8,128]{3,2,1,0:T(8,128)(2,1)} %get-tuple-element.630), channel_id=1, source_target_pairs={{32,0},{64,32},{96,64},{128,96},{160,128},{192,160},{224,192},{33,... | collective-permute-start | bytes 196616 | tf_op jit(solution)/shard_map/while/body/eval_jaxpr/ppermute | solution.py:10
  337.1 6.0 %collective-permute-start.1 = (bf16[4,8,8,128]{3,2,1,0:T(8,128)(2,1)}, bf16[4,8,8,128]{3,2,1,0:T(8,128)(2,1)}, u32[]{:S(2)}, u32[]{:S(2)}) collective-permute-start(bf16[4,8,8,128]{3,2,1,0:T(8,128)(2,1)} %get-tuple-element.630), channel_id=1, source_target_pairs={{32,0},{64,32},{96,64},{128,96},{160,128},{192,160},{224,192},{33,... | collective-permute-start | bytes 196616 | tf_op jit(solution)/shard_map/while/body/eval_jaxpr/ppermute | solution.py:10
  348.4 6.0 %collective-permute-start.1 = (bf16[4,8,8,128]{3,2,1,0:T(8,128)(2,1)}, bf16[4,8,8,128]{3,2,1,0:T(8,128)(2,1)}, u32[]{:S(2)}, u32[]{:S(2)}) collective-permute-start(bf16[4,8,8,128]{3,2,1,0:T(8,128)(2,1)} %get-tuple-element.630), channel_id=1, source_target_pairs={{32,0},{64,32},{96,64},{128,96},{160,128},{192,160},{224,192},{33,... | collective-permute-start | bytes 196616 | tf_op jit(solution)/shard_map/while/body/eval_jaxpr/ppermute | solution.py:10
  359.7 6.0 %collective-permute-start.1 = (bf16[4,8,8,128]{3,2,1,0:T(8,128)(2,1)}, bf16[4,8,8,128]{3,2,1,0:T(8,128)(2,1)}, u32[]{:S(2)}, u32[]{:S(2)}) collective-permute-start(bf16[4,8,8,128]{3,2,1,0:T(8,128)(2,1)} %get-tuple-element.630), channel_id=1, source_target_pairs={{32,0},{64,32},{96,64},{128,96},{160,128},{192,160},{224,192},{33,... | collective-permute-start | bytes 196616 | tf_op jit(solution)/shard_map/while/body/eval_jaxpr/ppermute | solution.py:10
  371.0 6.0 %collective-permute-start.1 = (bf16[4,8,8,128]{3,2,1,0:T(8,128)(2,1)}, bf16[4,8,8,128]{3,2,1,0:T(8,128)(2,1)}, u32[]{:S(2)}, u32[]{:S(2)}) collective-permute-start(bf16[4,8,8,128]{3,2,1,0:T(8,128)(2,1)} %get-tuple-element.630), channel_id=1, source_target_pairs={{32,0},{64,32},{96,64},{128,96},{160,128},{192,160},{224,192},{33,... | collective-permute-start | bytes 196616 | tf_op jit(solution)/shard_map/while/body/eval_jaxpr/ppermute | solution.py:10
  498.3 10.7 %collective-permute-start.2 = (bf16[112,128]{1,0:T(8,128)(2,1)S(1)}, bf16[112,128]{1,0:T(8,128)(2,1)S(1)}, u32[]{:S(2)}, u32[]{:S(2)}) collective-permute-start(bf16[112,128]{1,0:T(8,128)(2,1)S(1)} %fusion), channel_id=1, source_target_pairs={{0,1},{1,2},{2,3},{3,4},{4,5},{5,6},{6,7},{7,8},{8,9},{9,10},{10,1... | collective-permute-start | bytes 86024
  500.3 7.6 %collective-permute-start.3 = (bf16[12,128]{1,0:T(8,128)(2,1)S(1)}, bf16[12,128]{1,0:T(8,128)(2,1)S(1)}, u32[]{:S(2)}, u32[]{:S(2)}) collective-permute-start(bf16[12,128]{1,0:T(8,128)(2,1)S(1)} %slice.589), channel_id=1, source_target_pairs={{0,2},{1,3},{2,4},{3,5},{4,6},{5,7},{6,8},{7,9},{8,10},{9,11},{10,... | collective-permute-start | bytes 9224
  (18 other events, 174.3 us)
